TPU v7x, 32 devices: a whole 2x2x4 slice. The times are simulated.
32 devices in a mesh: parts: 2 (over x), row: 16 (over z, y, core).
Axes of the slice: x: 2, y: 2, z: 4, core: 2. Of those that a mesh axis runs over, the one named last changes fastest.
Arguments:
- embeddings: bfloat16 [16384, 512], P(('parts', 'row')), parts along dimension 0, may hold values from -6 to 6
- sizes: int32 [64], P('parts'), parts along dimension 0, may hold values from 1 to 2048, 8192 in all
- order: int32 [16384], P('parts'), parts along dimension 0, may hold values from 0 to 8191, each once
Outputs:
- similarity: float32 [16384], P(('parts', 'row')), parts along dimension 0
There are 2 independent parts, one for each index of `parts`. A program takes and returns all parts, laid end to end along the dimension named above; each array names one. Nothing has to cross between parts.
Inputs may be any that keep to these rules, and one draw needn't show every extreme that they name: `sizes`: each cluster has 1 to 2048 items; they sum to 8192. `order`: each of 0 to 8191 once.
All inputs are finite; a program needn't handle non-finite values.
Results may differ from a plain program's by a relative error of at most 0.0014.
Values may be sent and summed in bfloat16 or wider, within the bound.
A program may use at most 64 MiB of HBM per device.

v0:
```python
import jax
import jax.numpy as jnp
from jax import lax
from jax.sharding import PartitionSpec as P

REACH = 4


def shifted(x, axis, by):
    devices = lax.axis_size(axis)
    pairs = [(i, i + by) for i in range(devices) if 0 <= i + by < devices]
    return lax.ppermute(x, axis, pairs)


def cluster_of(ends, first, count):
    index = first + jnp.arange(count, dtype=jnp.int32)
    return jnp.sum((index[:, None] >= ends[None, :]).astype(jnp.int32), axis=1)


def local(embeddings, sizes, order):
    rows = embeddings.shape[0]
    devices = lax.axis_size("row")
    me = lax.axis_index("row")
    values = embeddings.astype(jnp.float32)
    unit = (values * lax.rsqrt(jnp.sum(values * values, axis=1, keepdims=True) + 1e-06)).astype(
        jnp.bfloat16
    )
    ends = jnp.cumsum(sizes)
    own_start = me * rows
    own_cluster = cluster_of(ends, own_start, rows)
    own_order = lax.dynamic_slice_in_dim(order, own_start, rows, 0)
    empty = jnp.full((rows,), -1.0, jnp.float32)
    count = unit.shape[0]
    update_scores = jnp.dot(unit, unit.T, preferred_element_type=jnp.float32)
    update_other = cluster_of(ends, own_start, count)
    update_ranks = lax.dynamic_slice_in_dim(order, own_start, count, 0)
    keep = (
        (own_cluster[:, None] == update_other[None, :])
        & (update_ranks[None, :] < own_order[:, None])
        & True
    )
    best = jnp.maximum(empty, jnp.max(jnp.where(keep, update_scores, jnp.float32(-1.0)), axis=1))
    for offset in range(1, REACH + 1):
        piece = shifted(unit, "row", offset)
        source = me - offset
        valid = source >= 0
        start = jnp.clip(source, 0, devices - 1) * rows
        scores = jnp.dot(unit, piece.T, preferred_element_type=jnp.float32)
        other = cluster_of(ends, start, rows)
        ranks = lax.dynamic_slice_in_dim(order, start, rows, 0)
        same = (own_cluster[:, None] == other[None, :]) & valid
        mine_keep = same & (ranks[None, :] < own_order[:, None])
        their_keep = same & (own_order[:, None] < ranks[None, :])
        best = jnp.maximum(best, jnp.max(jnp.where(mine_keep, scores, jnp.float32(-1.0)), axis=1))
        partner = jnp.max(jnp.where(their_keep, scores, jnp.float32(-1.0)), axis=0)
        returned = shifted(partner, "row", -offset)
        arrived = me + offset < devices
        best = jnp.maximum(best, jnp.where(arrived, returned, jnp.float32(-1.0)))
    return best


def solution(mesh):
    return jax.shard_map(
        local,
        mesh=mesh,
        in_specs=(P(("parts", "row"), None), P("parts"), P("parts")),
        out_specs=P(("parts", "row")),
        check_vma=False,
    )
```

profile of v0, /device:TPU:12, one launch (start us, length us, event | category | flops | bytes accessed | tf_op | source)
XLA Modules:
  0.0 61.9 jit_solution(5973600296252474014)
XLA Ops:
  0.0 1.3 %fusion.1 = f32[512]{0:T(512)S(1)} fusion(bf16[512,512]{1,0:T(8,128)(2,1)} %param.3), kind=kLoop, calls=%fused_computation.4 | loop fusion | flops 785920 | bytes 526336 | tf_op jit(solution)/shard_map/reduce_sum | solution.py:25
  1.3 0.0 copy-done
  1.3 0.2 fusion.2
  1.5 2.9 %collective-permute-start.4 = (bf16[512,512]{1,0:T(8,128)(2,1)S(1)}, bf16[512,512]{1,0:T(8,128)(2,1)S(1)}, u32[]{:S(2)}, u32[]{:S(2)}) collective-permute-start(bf16[512,512]{1,0:T(8,128)(2,1)S(1)} %fusion.2), channel_id=1, source_target_pairs={{0,3},{1,4},{2,5},{3,6},{4,7},{5,8},{6,9},{7,10},{8,11},{9,12},{10... | collective-permute-start | bytes 1572872 | tf_op jit(solution)/shard_map/ppermute | solution.py:12
  4.4 3.5 %collective-permute-start.6 = (bf16[512,512]{1,0:T(8,128)(2,1)S(1)}, bf16[512,512]{1,0:T(8,128)(2,1)S(1)}, u32[]{:S(2)}, u32[]{:S(2)}) collective-permute-start(bf16[512,512]{1,0:T(8,128)(2,1)S(1)} %fusion.2), channel_id=1, source_target_pairs={{0,4},{1,5},{2,6},{3,7},{4,8},{5,9},{6,10},{7,11},{8,12},{9,13},{1... | collective-permute-start | bytes 1572872 | tf_op jit(solution)/shard_map/ppermute | solution.py:12
  7.9 3.4 %collective-permute-start.2 = (bf16[512,512]{1,0:T(8,128)(2,1)S(1)}, bf16[512,512]{1,0:T(8,128)(2,1)S(1)}, u32[]{:S(2)}, u32[]{:S(2)}) collective-permute-start(bf16[512,512]{1,0:T(8,128)(2,1)S(1)} %fusion.2), channel_id=1, source_target_pairs={{0,2},{1,3},{2,4},{3,5},{4,6},{5,7},{6,8},{7,9},{8,10},{9,11},{10,... | collective-permute-start | bytes 1572872 | tf_op jit(solution)/shard_map/ppermute | solution.py:12
  11.3 1.9 %collective-permute-start = (bf16[512,512]{1,0:T(8,128)(2,1)S(1)}, bf16[512,512]{1,0:T(8,128)(2,1)S(1)}, u32[]{:S(2)}, u32[]{:S(2)}) collective-permute-start(bf16[512,512]{1,0:T(8,128)(2,1)S(1)} %fusion.2), channel_id=1, source_target_pairs={{0,1},{1,2},{2,3},{3,4},{4,5},{5,6},{6,7},{7,8},{8,9},{9,10},{10,1... | collective-permute-start | bytes 1572872 | tf_op jit(solution)/shard_map/ppermute | solution.py:12
  13.3 0.0 copy-start.1
  13.3 0.6 %copy-done.1 = s32[32]{0:T(128)S(1)} copy-done((s32[32]{0:T(128)S(1)}, s32[32]{0:T(128)}, u32[]{:S(2)}) %copy-start.1) | copy-done | bytes 152
  14.0 0.1 copy.22
  14.0 0.1 reduce-window.8
  14.1 0.1 reduce
  14.2 0.9 %fusion.3 = (s32[512]{0:T(512)S(1)}, s32[512]{0:T(512)S(1)}, s32[512]{0:T(512)S(1)}, s32[512]{0:T(512)S(1)}, s32[512]{0:T(512)S(1)}) fusion(s32[8192]{0:T(1024)} %param.5, s32[]{:T(128)S(6)} %select_n.87, s32[]{:T(128)S(6)} %select_n.77, s32[]{:T(128)S(6)} %select_n.72, s32[]{:T(128)S(6)} %select_n.70, s32[]{:T(128)S(6)} %select_n.82), kind=kLoop, calls=%fused_computation.30 | loop fusion | bytes 20500 | tf_op jit(solution)/shard_map/dynamic_slice | solution.py:50
  15.1 0.1 convert_reduce_fusion.3
  15.2 2.4 %collective-permute-done.4 = bf16[512,512]{1,0:T(8,128)(2,1)S(1)} collective-permute-done((bf16[512,512]{1,0:T(8,128)(2,1)S(1)}, bf16[512,512]{1,0:T(8,128)(2,1)S(1)}, u32[]{:S(2)}, u32[]{:S(2)}) %collective-permute-start.4) | collective-permute-done | bytes 524320 | tf_op jit(solution)/shard_map/ppermute | solution.py:12
  17.6 0.5 fusion.5
  18.1 10.7 %collective-permute-done.6 = bf16[512,512]{1,0:T(8,128)(2,1)S(1)} collective-permute-done((bf16[512,512]{1,0:T(8,128)(2,1)S(1)}, bf16[512,512]{1,0:T(8,128)(2,1)S(1)}, u32[]{:S(2)}, u32[]{:S(2)}) %collective-permute-start.6) | collective-permute-done | bytes 524320 | tf_op jit(solution)/shard_map/ppermute | solution.py:12
  28.8 0.5 fusion.6
  29.2 9.9 %collective-permute-done.2 = bf16[512,512]{1,0:T(8,128)(2,1)S(1)} collective-permute-done((bf16[512,512]{1,0:T(8,128)(2,1)S(1)}, bf16[512,512]{1,0:T(8,128)(2,1)S(1)}, u32[]{:S(2)}, u32[]{:S(2)}) %collective-permute-start.2) | collective-permute-done | bytes 524320 | tf_op jit(solution)/shard_map/ppermute | solution.py:12
  39.1 0.5 fusion.4
  39.6 0.0 collective-permute-done
  39.6 3.0 %select_reduce_fusion.7 = (f32[512]{0:T(512)S(1)}, f32[512]{0:T(512)S(1)}, f32[512]{0:T(512)S(1)}, f32[512]{0:T(512)S(1)}, f32[512]{0:T(512)S(1)}, /*index=5*/f32[512]{0:T(512)S(1)}, f32[512]{0:T(512)S(1)}, f32[512]{0:T(512)S(1)}) fusion(s32[512]{0:T(512)S(1)} %get-tuple-element.27, s32[512]{0:T(512)S(1)} %get-tuple-element.23, ...), kind=kOutput, calls=%fused_computation.13 | convolution fusion | flops 278917120 | bytes 4231172 | tf_op jit(solution)/shard_map/dot_general | solution.py:48
  42.6 4.0 %collective-permute-start.1 = (f32[512]{0:T(512)S(1)}, f32[512]{0:T(512)S(1)}, u32[]{:S(2)}, u32[]{:S(2)}) collective-permute-start(f32[512]{0:T(512)S(1)} %get-tuple-element.6), channel_id=1, source_target_pairs={{1,0},{2,1},{3,2},{4,3},{5,4},{6,5},{7,6},{8,7},{9,8},{10,9},{11,1... | collective-permute-start | bytes 6152 | tf_op jit(solution)/shard_map/ppermute | solution.py:12
  46.6 7.4 %collective-permute-start.3 = (f32[512]{0:T(512)S(1)}, f32[512]{0:T(512)S(1)}, u32[]{:S(2)}, u32[]{:S(2)}) collective-permute-start(f32[512]{0:T(512)S(1)} %get-tuple-element.13), channel_id=1, source_target_pairs={{2,0},{3,1},{4,2},{5,3},{6,4},{7,5},{8,6},{9,7},{10,8},{11,9},{12,... | collective-permute-start | bytes 6152 | tf_op jit(solution)/shard_map/ppermute | solution.py:12
  53.9 1.9 %collective-permute-start.5 = (f32[512]{0:T(512)S(1)}, f32[512]{0:T(512)S(1)}, u32[]{:S(2)}, u32[]{:S(2)}) collective-permute-start(f32[512]{0:T(512)S(1)} %get-tuple-element.15), channel_id=1, source_target_pairs={{3,0},{4,1},{5,2},{6,3},{7,4},{8,5},{9,6},{10,7},{11,8},{12,9},{13... | collective-permute-start | bytes 6152 | tf_op jit(solution)/shard_map/ppermute | solution.py:12
  55.9 1.9 %collective-permute-start.7 = (f32[512]{0:T(512)S(1)}, f32[512]{0:T(512)S(1)}, u32[]{:S(2)}, u32[]{:S(2)}) collective-permute-start(f32[512]{0:T(512)S(1)} %get-tuple-element.17), channel_id=1, source_target_pairs={{4,0},{5,1},{6,2},{7,3},{8,4},{9,5},{10,6},{11,7},{12,8},{13,9},{1... | collective-permute-start | bytes 6152 | tf_op jit(solution)/shard_map/ppermute | solution.py:12
  57.8 0.5 fusion
  58.3 0.0 collective-permute-done.1
  58.3 0.0 collective-permute-done.3
  58.3 1.4 %collective-permute-done.5 = f32[512]{0:T(512)S(1)} collective-permute-done((f32[512]{0:T(512)S(1)}, f32[512]{0:T(512)S(1)}, u32[]{:S(2)}, u32[]{:S(2)}) %collective-permute-start.5) | collective-permute-done | bytes 2080 | tf_op jit(solution)/shard_map/ppermute | solution.py:12
  59.7 1.6 %collective-permute-done.7 = f32[512]{0:T(512)S(1)} collective-permute-done((f32[512]{0:T(512)S(1)}, f32[512]{0:T(512)S(1)}, u32[]{:S(2)}, u32[]{:S(2)}) %collective-permute-start.7) | collective-permute-done | bytes 2080 | tf_op jit(solution)/shard_map/ppermute | solution.py:12
  61.3 0.6 select_maximum_fusion
  (5 shorter events, 0.0 us)
Async XLA Ops:
  0.0 1.3 %copy-start = (bf16[512,512]{1,0:T(8,128)(2,1)S(1)}, bf16[512,512]{1,0:T(8,128)(2,1)}, u32[]{:S(2)}) copy-start(bf16[512,512]{1,0:T(8,128)(2,1)} %param.3) | copy-start | bytes 1572868
  1.5 16.1 %collective-permute-start.4 = (bf16[512,512]{1,0:T(8,128)(2,1)S(1)}, bf16[512,512]{1,0:T(8,128)(2,1)S(1)}, u32[]{:S(2)}, u32[]{:S(2)}) collective-permute-start(bf16[512,512]{1,0:T(8,128)(2,1)S(1)} %fusion.2), channel_id=1, source_target_pairs={{0,3},{1,4},{2,5},{3,6},{4,7},{5,8},{6,9},{7,10},{8,11},{9,12},{10... | collective-permute-start | bytes 1572872 | tf_op jit(solution)/shard_map/ppermute | solution.py:12
  4.4 24.4 %collective-permute-start.6 = (bf16[512,512]{1,0:T(8,128)(2,1)S(1)}, bf16[512,512]{1,0:T(8,128)(2,1)S(1)}, u32[]{:S(2)}, u32[]{:S(2)}) collective-permute-start(bf16[512,512]{1,0:T(8,128)(2,1)S(1)} %fusion.2), channel_id=1, source_target_pairs={{0,4},{1,5},{2,6},{3,7},{4,8},{5,9},{6,10},{7,11},{8,12},{9,13},{1... | collective-permute-start | bytes 1572872 | tf_op jit(solution)/shard_map/ppermute | solution.py:12
  7.9 31.2 %collective-permute-start.2 = (bf16[512,512]{1,0:T(8,128)(2,1)S(1)}, bf16[512,512]{1,0:T(8,128)(2,1)S(1)}, u32[]{:S(2)}, u32[]{:S(2)}) collective-permute-start(bf16[512,512]{1,0:T(8,128)(2,1)S(1)} %fusion.2), channel_id=1, source_target_pairs={{0,2},{1,3},{2,4},{3,5},{4,6},{5,7},{6,8},{7,9},{8,10},{9,11},{10,... | collective-permute-start | bytes 1572872 | tf_op jit(solution)/shard_map/ppermute | solution.py:12
  11.3 28.3 %collective-permute-start = (bf16[512,512]{1,0:T(8,128)(2,1)S(1)}, bf16[512,512]{1,0:T(8,128)(2,1)S(1)}, u32[]{:S(2)}, u32[]{:S(2)}) collective-permute-start(bf16[512,512]{1,0:T(8,128)(2,1)S(1)} %fusion.2), channel_id=1, source_target_pairs={{0,1},{1,2},{2,3},{3,4},{4,5},{5,6},{6,7},{7,8},{8,9},{9,10},{10,1... | collective-permute-start | bytes 1572872 | tf_op jit(solution)/shard_map/ppermute | solution.py:12
  13.3 0.7 %copy-start.1 = (s32[32]{0:T(128)S(1)}, s32[32]{0:T(128)}, u32[]{:S(2)}) copy-start(s32[32]{0:T(128)} %param.4) | copy-start | bytes 388
  42.6 15.8 %collective-permute-start.1 = (f32[512]{0:T(512)S(1)}, f32[512]{0:T(512)S(1)}, u32[]{:S(2)}, u32[]{:S(2)}) collective-permute-start(f32[512]{0:T(512)S(1)} %get-tuple-element.6), channel_id=1, source_target_pairs={{1,0},{2,1},{3,2},{4,3},{5,4},{6,5},{7,6},{8,7},{9,8},{10,9},{11,1... | collective-permute-start | bytes 6152 | tf_op jit(solution)/shard_map/ppermute | solution.py:12
  46.6 11.8 %collective-permute-start.3 = (f32[512]{0:T(512)S(1)}, f32[512]{0:T(512)S(1)}, u32[]{:S(2)}, u32[]{:S(2)}) collective-permute-start(f32[512]{0:T(512)S(1)} %get-tuple-element.13), channel_id=1, source_target_pairs={{2,0},{3,1},{4,2},{5,3},{6,4},{7,5},{8,6},{9,7},{10,8},{11,9},{12,... | collective-permute-start | bytes 6152 | tf_op jit(solution)/shard_map/ppermute | solution.py:12
  53.9 5.8 %collective-permute-start.5 = (f32[512]{0:T(512)S(1)}, f32[512]{0:T(512)S(1)}, u32[]{:S(2)}, u32[]{:S(2)}) collective-permute-start(f32[512]{0:T(512)S(1)} %get-tuple-element.15), channel_id=1, source_target_pairs={{3,0},{4,1},{5,2},{6,3},{7,4},{8,5},{9,6},{10,7},{11,8},{12,9},{13... | collective-permute-start | bytes 6152 | tf_op jit(solution)/shard_map/ppermute | solution.py:12
  55.9 5.5 %collective-permute-start.7 = (f32[512]{0:T(512)S(1)}, f32[512]{0:T(512)S(1)}, u32[]{:S(2)}, u32[]{:S(2)}) collective-permute-start(f32[512]{0:T(512)S(1)} %get-tuple-element.17), channel_id=1, source_target_pairs={{4,0},{5,1},{6,2},{7,3},{8,4},{9,5},{10,6},{11,7},{12,8},{13,9},{1... | collective-permute-start | bytes 6152 | tf_op jit(solution)/shard_map/ppermute | solution.py:12
where the time goes:
time: 62.8 us; the launch traced here: 61.9 us
  starting transfers between devices  26.9 us (43%)
  waiting for transfers between devices  25.9 us (41%)
  matrix products  4.92 us (8%)
  other arithmetic  2.37 us (4%)
  local copies, waits for them, and re-layouts  1.6 us (3%)
    ppermute x8, starting transfers between devices, shifted(): return lax.ppermute(x, axis, pairs)  26.9 us
    ppermute x8, waiting for transfers between devices, shifted(): return lax.ppermute(x, axis, pairs)  25.9 us
    dot_general x4, matrix products, local(): scores = jnp.dot(unit, piece.T, preferred_element_type=jnp.float32)  4.4 us
    reduce_sum x1, other arithmetic, local(): jnp.sum(values * values, axis=1, keepdims=True) + 1e-06  1.29 us
  transfers between devices with their start and end apart: 8, of which 5 were waited for; matrix products, arithmetic and copies ran while one was open for 5% of the time, Pallas kernels for 0%

commit v1 on v0

v1 whole, which is shorter than its diff:
```python
import functools

import jax
import jax.numpy as jnp
from jax import lax
from jax.experimental import pallas as pl
from jax.experimental.pallas import tpu as pltpu
from jax.sharding import PartitionSpec as P

OWN, PART, ZED, WHY, FAR = range(5)
LANES = 128
CHUNKS = 4
BIG = 1e9
MESH = pl.DeviceIdType.MESH


def kernel(devices, x_ref, sizes_ref, order_ref, out_ref, raw, unit, col, acc_low, acc_high, ret, back,
           load_sem, send_sem, recv_sem, ret_send, ret_recv):
    rows, width = x_ref.shape
    tiles = rows // LANES
    piece = rows // CHUNKS
    clusters = sizes_ref.shape[0]
    parts_at = lax.axis_index("parts")
    me = lax.axis_index("row")
    core = lax.rem(me, 2)
    is_b = lax.rem(me // 2, 2)
    is_a = 1 - is_b
    plane = me // 4
    planes = devices // 4
    partner = me + 1 - 2 * core
    has_down = plane > 0
    has_up = plane < planes - 1
    other_chip = me - core + 2 - 4 * is_b

    def dev(index):
        return (parts_at, index)

    def both(*conditions):
        result = conditions[0]
        for condition in conditions[1:]:
            result = jnp.logical_and(result, condition)
        return result

    on_a, on_b = is_a == 1, is_b == 1
    first, second = core == 0, core == 1

    barrier = pltpu.get_barrier_semaphore()

    def greet(index):
        pl.semaphore_signal(barrier, inc=1, device_id=dev(index), device_id_type=MESH)

    greet(partner)
    greet(other_chip)
    greet(other_chip + 1)
    pl.when(has_down)(lambda: greet(me - 4))
    pl.when(has_up)(lambda: greet(me + 4))
    load = pltpu.make_async_copy(x_ref, raw.at[OWN], load_sem)
    load.start()
    pl.semaphore_wait(barrier, 3 + has_down.astype(jnp.int32) + has_up.astype(jnp.int32))

    def chunk(c):
        return pl.ds(c * piece, piece)

    def own_copy(slot, c, target):
        return pltpu.make_async_remote_copy(
            src_ref=x_ref.at[chunk(c)], dst_ref=raw.at[slot, chunk(c)],
            send_sem=send_sem.at[slot, c], recv_sem=recv_sem.at[slot, c],
            device_id=dev(target), device_id_type=MESH)

    def far_copy(c):
        return pltpu.make_async_remote_copy(
            src_ref=raw.at[WHY, chunk(c)], dst_ref=raw.at[FAR, chunk(c)],
            send_sem=send_sem.at[FAR, c], recv_sem=recv_sem.at[FAR, c],
            device_id=dev(partner), device_id_type=MESH)

    def part_copy():
        return pltpu.make_async_remote_copy(
            src_ref=x_ref, dst_ref=raw.at[PART],
            send_sem=send_sem.at[PART, 0], recv_sem=recv_sem.at[PART, 0],
            device_id=dev(partner), device_id_type=MESH)

    def ret_copy(slot, target):
        return pltpu.make_async_remote_copy(
            src_ref=back.at[slot], dst_ref=ret.at[slot],
            send_sem=ret_send.at[slot], recv_sem=ret_recv.at[slot],
            device_id=dev(target), device_id_type=MESH)

    z_target = jnp.where(on_b, me + 4, me - 4)
    z_source = jnp.where(on_b, me - 4, me + 4)
    sends_z = jnp.where(on_b, has_up, has_down)
    takes_z = jnp.where(on_b, has_down, has_up)
    sends_part = core == is_a
    takes_part = core == is_b
    sent = []

    for c in range(CHUNKS):
        @pl.when(sends_z)
        def _():
            own_copy(ZED, c, z_target).start()

        @pl.when(on_a)
        def _():
            own_copy(WHY, c, me + 2).start()

    @pl.when(sends_part)
    def _():
        part_copy().start()

    base = me - core - 2 * is_b
    block_of = [me, partner, z_source, base + core, base + 1 - core]
    sub = lax.broadcasted_iota(jnp.int32, (8, LANES), 0)
    lane = lax.broadcasted_iota(jnp.int32, (8, LANES), 1)
    last = jnp.zeros((8, LANES), jnp.int32)
    for slot, block in enumerate(block_of):
        last = jnp.where(sub == slot, (block + 1) * rows - 1, last)
    mine = me * rows + sub * LANES + lane

    def scan(c, carry):
        end, begin_last, end_last, begin_mine, end_mine = carry
        end = end + sizes_ref[c]
        done = end <= last
        begin_last = jnp.where(done, end, begin_last)
        end_last = jnp.where(done, end_last, jnp.minimum(end_last, end))
        done = end <= mine
        begin_mine = jnp.where(done, end, begin_mine)
        end_mine = jnp.where(done, end_mine, jnp.minimum(end_mine, end))
        return end, begin_last, end_last, begin_mine, end_mine

    zero = jnp.zeros((8, LANES), jnp.int32)
    top = jnp.full((8, LANES), 1 << 30, jnp.int32)
    carry = (jnp.int32(0), zero, top, zero, top)
    carry = lax.fori_loop(0, clusters, scan, carry, unroll=8)
    _, begin_last, end_last, begin_mine, end_mine = carry
    low = [begin_last[s:s + 1] for s in range(5)]
    high = [end_last[s:s + 1] for s in range(5)]
    lane_row = lax.broadcasted_iota(jnp.int32, (1, LANES), 1)

    def index_row(slot, t):
        return block_of[slot] * rows + t * LANES + lane_row

    def clipped(slot):
        return jnp.clip(block_of[slot], 0, devices - 1)

    def rank_row(slot, t):
        return order_ref[pl.ds(clipped(slot) * tiles + t, 1), :].astype(jnp.float32)

    def spread(row):
        return jnp.transpose(jnp.broadcast_to(row, (LANES, LANES)))

    for slot in range(5):
        for t in range(tiles):
            row = jnp.where(index_row(slot, t) >= low[slot], rank_row(slot, t), BIG)
            col[slot, pl.ds(t * LANES, LANES), :] = spread(row)
    for t in range(tiles):
        col[5, pl.ds(t * LANES, LANES), :] = spread(rank_row(OWN, t))
    acc_low[...] = jnp.full(acc_low.shape, -1.0, jnp.float32)
    acc_high[...] = jnp.full(acc_high.shape, -1.0, jnp.float32)

    def normalize(slot, start, count):
        at = pl.ds(start, count)
        values = raw[slot, at, :].astype(jnp.float32)
        total = jnp.sum(values * values, axis=1, keepdims=True)
        unit[slot, at, :] = (values * lax.rsqrt(total + 1e-06)).astype(jnp.bfloat16)

    def dot(a, b):
        return lax.dot_general(a, b, (((1,), (1,)), ((), ())), preferred_element_type=jnp.float32)

    def fold(x):
        return jnp.max(x.reshape(x.shape[0] // 8, 8, x.shape[1]), axis=0)

    def pair(lower, start, count, higher, first_col, cols):
        others = unit[higher, pl.ds(first_col, cols), :]
        ranks, inside = [], []
        for t in range(first_col // LANES, (first_col + cols) // LANES):
            within = index_row(higher, t) < high[lower]
            inside.append(within)
            ranks.append(jnp.where(within, rank_row(higher, t), 2 * BIG))

        def step(i, carry):
            at = pl.ds(pl.multiple_of(start + i * LANES, LANES), LANES)
            scores = dot(unit[lower, at, :], others)
            ranks_low = col[lower, at, :]
            best = acc_low[lower, at, :]
            result = []
            for n in range(len(ranks)):
                s = scores[:, n * LANES:(n + 1) * LANES]
                before = ranks_low < ranks[n]
                best = jnp.maximum(best, jnp.where(before, -1.0, s))
                result.append(jnp.maximum(carry[n], fold(jnp.where(before, s, -1.0))))
            acc_low[lower, at, :] = best
            return tuple(result)

        found = tuple(jnp.full((8, LANES), -1.0, jnp.float32) for _ in ranks)
        found = lax.fori_loop(0, count // LANES, step, found)
        for n in range(len(ranks)):
            at = pl.ds(first_col + n * LANES, LANES)
            masked = jnp.where(inside[n], found[n], -1.0)
            acc_high[higher, :, at] = jnp.maximum(acc_high[higher, :, at], masked)

    def within_own():
        others = unit[OWN]
        ranks = [rank_row(OWN, t) for t in range(tiles)]
        begins = [begin_mine[t:t + 1] for t in range(tiles)]
        ends = [end_mine[t:t + 1] for t in range(tiles)]

        def step(i, carry):
            at = pl.ds(pl.multiple_of(i * LANES, LANES), LANES)
            scores = dot(unit[OWN, at, :], others)
            ranks_low = col[5, at, :]
            index = me * rows + i * LANES + lax.broadcasted_iota(jnp.int32, (LANES, LANES), 0)
            result = []
            for n in range(tiles):
                s = scores[:, n * LANES:(n + 1) * LANES]
                keep = (ranks_low < ranks[n]) & (index >= begins[n]) & (index < ends[n])
                result.append(jnp.maximum(carry[n], fold(jnp.where(keep, s, -1.0))))
            return tuple(result)

        found = tuple(jnp.full((8, LANES), -1.0, jnp.float32) for _ in ranks)
        found = lax.fori_loop(0, tiles, step, found)
        for n in range(tiles):
            at = pl.ds(n * LANES, LANES)
            acc_high[OWN, :, at] = jnp.maximum(acc_high[OWN, :, at], found[n])

    def result_of(slot, lows=True):
        pieces = []
        for t in range(tiles):
            at = pl.ds(t * LANES, LANES)
            best = jnp.max(acc_high[slot, :, at], axis=0, keepdims=True)
            if lows:
                found = jnp.max(jnp.transpose(acc_low[slot, at, :]), axis=0, keepdims=True)
                best = jnp.maximum(best, jnp.where(index_row(slot, t) >= low[slot], found, -1.0))
            pieces.append(best)
        return jnp.concatenate(pieces, axis=1)

    load.wait()
    normalize(OWN, 0, rows)
    within_own()

    @pl.when(takes_part)
    def _():
        part_copy().wait_recv()
        normalize(PART, 0, rows)

    @pl.when(both(on_b, second))
    def _():
        pair(PART, 0, rows, OWN, 0, rows)

    @pl.when(both(on_a, first))
    def _():
        pair(OWN, 0, rows, PART, 0, rows)

    @pl.when(on_b)
    def _():
        for c in range(CHUNKS):
            start = c * piece
            own_copy(WHY, c, partner).wait_recv()
            far_copy(c).start()
            normalize(WHY, start, piece)
            pair(WHY, start, piece, OWN, 0, rows)

            @pl.when(has_down)
            def _():
                own_copy(ZED, c, partner).wait_recv()
                normalize(ZED, start, piece)
                pair(ZED, start, piece, OWN, 0, rows)

                @pl.when(second)
                def _():
                    pair(ZED, start, piece, PART, 0, rows)

                pair(ZED, start, piece, WHY, 0, start + piece)
                if c:
                    pair(ZED, 0, start, WHY, start, piece)

            far_copy(c).wait_recv()
            normalize(FAR, start, piece)
            pair(FAR, start, piece, OWN, 0, rows)

            @pl.when(has_down)
            def _():
                pair(ZED, start, piece, FAR, 0, start + piece)
                if c:
                    pair(ZED, 0, start, FAR, start, piece)

        back[2] = result_of(WHY)
        back[3] = result_of(FAR)

        @pl.when(first)
        def _():
            ret_copy(2, me - 2).start()
            pltpu.make_async_remote_copy(
                src_ref=back.at[3], dst_ref=ret.at[2], send_sem=ret_send.at[3], recv_sem=ret_recv.at[2],
                device_id=dev(me - 1), device_id_type=MESH).start()

        @pl.when(second)
        def _():
            pltpu.make_async_remote_copy(
                src_ref=back.at[2], dst_ref=ret.at[3], send_sem=ret_send.at[2], recv_sem=ret_recv.at[3],
                device_id=dev(me - 2), device_id_type=MESH).start()
            ret_copy(3, me - 3).start()
            back[1] = result_of(PART)
            ret_copy(1, partner).start()

        @pl.when(has_down)
        def _():
            back[0] = result_of(ZED)
            ret_copy(0, me - 4).start()

    @pl.when(on_a)
    def _():
        @pl.when(has_up)
        def _():
            for c in range(CHUNKS):
                start = c * piece
                own_copy(ZED, c, partner).wait_recv()
                normalize(ZED, start, piece)
                pair(OWN, 0, rows, ZED, start, piece)

                @pl.when(first)
                def _():
                    pair(PART, 0, rows, ZED, start, piece)

            back[0] = result_of(ZED, False)
            ret_copy(0, me + 4).start()

        @pl.when(first)
        def _():
            back[1] = result_of(PART)
            ret_copy(1, partner).start()

    out_ref[...] = result_of(OWN)

    def take(slot):
        ret_copy(slot, partner).wait_recv()
        out_ref[...] = jnp.maximum(out_ref[...], ret[slot])

    pl.when(sends_part)(lambda: take(1))
    pl.when(sends_z)(lambda: take(0))

    @pl.when(on_a)
    def _():
        take(2)
        take(3)

    for c in range(CHUNKS):
        pl.when(sends_z)(lambda: own_copy(ZED, c, partner).wait_send())
        pl.when(on_a)(lambda: own_copy(WHY, c, partner).wait_send())
        pl.when(on_b)(lambda: far_copy(c).wait_send())
    pl.when(sends_part)(lambda: part_copy().wait_send())
    pl.when(takes_part)(lambda: ret_copy(1, partner).wait_send())
    pl.when(takes_z)(lambda: ret_copy(0, partner).wait_send())

    @pl.when(on_b)
    def _():
        ret_copy(2, partner).wait_send()
        ret_copy(3, partner).wait_send()


def local(embeddings, sizes, order, devices):
    rows, width = embeddings.shape
    order = order.reshape(-1, LANES)
    result = pl.pallas_call(
        functools.partial(kernel, devices),
        out_shape=jax.ShapeDtypeStruct((1, rows), jnp.float32),
        in_specs=[
            pl.BlockSpec(memory_space=pl.ANY),
            pl.BlockSpec(memory_space=pltpu.SMEM),
            pl.BlockSpec(memory_space=pltpu.VMEM),
        ],
        out_specs=pl.BlockSpec(memory_space=pltpu.VMEM),
        scratch_shapes=[
            pltpu.VMEM((5, rows, width), jnp.bfloat16),
            pltpu.VMEM((5, rows, width), jnp.bfloat16),
            pltpu.VMEM((6, rows, LANES), jnp.float32),
            pltpu.VMEM((5, rows, LANES), jnp.float32),
            pltpu.VMEM((5, 8, rows), jnp.float32),
            pltpu.VMEM((4, 1, rows), jnp.float32),
            pltpu.VMEM((4, 1, rows), jnp.float32),
            pltpu.SemaphoreType.DMA,
            pltpu.SemaphoreType.DMA((5, CHUNKS)),
            pltpu.SemaphoreType.DMA((5, CHUNKS)),
            pltpu.SemaphoreType.DMA((4,)),
            pltpu.SemaphoreType.DMA((4,)),
        ],
        compiler_params=pltpu.CompilerParams(collective_id=0, has_side_effects=True),
    )(embeddings, sizes, order)
    return result.reshape(rows)


def solution(mesh):
    return jax.shard_map(
        functools.partial(local, devices=mesh.shape["row"]),
        mesh=mesh,
        in_specs=(P(("parts", "row"), None), P("parts"), P("parts")),
        out_specs=P(("parts", "row")),
        check_vma=False,
    )
```

time: 62.8 us -> 24.5 us (0.39)
  starting transfers between devices: 26.9 us -> 0 us
  waiting for transfers between devices: 25.9 us -> 0 us
  Pallas kernels: 0 us -> 22.9 us
  matrix products: 4.92 us -> 0 us
  other arithmetic: 2.37 us -> 0 us
    ppermute x8 -> x0, starting transfers between devices: 26.9 us -> none  [shifted(): return lax.ppermute(x, axis, pairs)]
    ppermute x8 -> x0, waiting for transfers between devices: 25.9 us -> none  [shifted(): return lax.ppermute(x, axis, pairs)]
    pallas_call x0 -> x1, Pallas kernels: none -> 22.9 us  [local(): pl.pallas_call(functools.partial(kernel, devices), out_shape=jax.ShapeDty...]
    dot_general x5 -> x0, matrix products: 4.92 us -> none  [the longest x4 4.4 us: local(): scores = jnp.dot(unit, piece.T, preferred_element_type=jnp.float32)]
    reduce_sum x2 -> x0, other arithmetic: 1.42 us -> none  [the longest x1 1.29 us: local(): jnp.sum(values * values, axis=1, keepdims=True) + 1e-06]
    dynamic_slice x1 -> x0, local copies, waits for them, and re-layouts: 0.85 us -> none  [local(): ranks = lax.dynamic_slice_in_dim(order, start, rows, 0)]
    unnamed x4 -> x1, local copies, waits for them, and re-layouts: 0.65 us -> 1.26 us
  transfers between devices with their start and end apart: 8 -> 0, of which waited for: 5 -> 0; matrix products, arithmetic and copies ran while one was open for 5% -> 0% of each run, Pallas kernels for 0% -> 0%
where the time goes in v1:
time: 24.5 us; the launch traced here: 24.2 us
  Pallas kernels  22.9 us (93%)
  local copies, waits for them, and re-layouts  1.26 us (5%)
    pallas_call x1, Pallas kernels, local(): pl.pallas_call(functools.partial(kernel, devices), out_shape=jax.ShapeDty...  22.9 us
    unnamed x1, local copies, waits for them, and re-layouts  1.26 us

profile of v1, /device:TPU:12, one launch (start us, length us, event | category | flops | bytes accessed | tf_op | source)
XLA Modules:
  0.0 24.2 jit_solution(7774937570665763395)
XLA Ops:
  0.0 22.9 %shard_map.37 = f32[1,512]{1,0:T(1,128)} custom-call(bf16[512,512]{1,0:T(8,128)(2,1)} %x_ref.1, s32[32]{0:T(128)} %sizes_ref.1, s32[64,128]{1,0:T(8,128)} %bitcast.2), custom_call_target="tpu_custom_call" | custom-call | tf_op jit(solution)/shard_map/pallas_call | solution.py:362
  22.9 1.3 %copy.5 = f32[512]{0:T(512)} copy(f32[512]{0:T(512)} %bitcast.3) | data formatting | bytes 4096

commit v2 on v1

--- a/solution.py
+++ b/solution.py
@@ -14,8 +14,8 @@
 MESH = pl.DeviceIdType.MESH
 
 
-def kernel(devices, x_ref, sizes_ref, order_ref, out_ref, raw, unit, col, acc_low, acc_high, ret, back,
-           load_sem, send_sem, recv_sem, ret_send, ret_recv):
+def kernel(devices, x_ref, sizes_hbm, order_hbm, out_ref, sizes_ref, order_ref, raw, unit, col, acc_low, acc_high, ret, back,
+           load_sem, small_sem, send_sem, recv_sem, ret_send, ret_recv):
     rows, width = x_ref.shape
     tiles = rows // LANES
     piece = rows // CHUNKS
@@ -56,6 +56,10 @@
     pl.when(has_up)(lambda: greet(me + 4))
     load = pltpu.make_async_copy(x_ref, raw.at[OWN], load_sem)
     load.start()
+    load_sizes = pltpu.make_async_copy(sizes_hbm, sizes_ref, small_sem.at[0])
+    load_sizes.start()
+    load_order = pltpu.make_async_copy(order_hbm, order_ref, small_sem.at[1])
+    load_order.start()
     pl.semaphore_wait(barrier, 3 + has_down.astype(jnp.int32) + has_up.astype(jnp.int32))
 
     def chunk(c):
@@ -105,6 +109,9 @@
     @pl.when(sends_part)
     def _():
         part_copy().start()
+
+    load_sizes.wait()
+    load_order.wait()
 
     base = me - core - 2 * is_b
     block_of = [me, partner, z_source, base + core, base + 1 - core]
@@ -272,6 +279,21 @@
                 if c:
                     pair(ZED, 0, start, WHY, start, piece)
 
+            if c == CHUNKS - 1:
+                back[2] = result_of(WHY)
+
+                @pl.when(first)
+                def _():
+                    ret_copy(2, me - 2).start()
+
+                @pl.when(second)
+                def _():
+                    pltpu.make_async_remote_copy(
+                        src_ref=back.at[2], dst_ref=ret.at[3], send_sem=ret_send.at[2],
+                        recv_sem=ret_recv.at[3], device_id=dev(me - 2), device_id_type=MESH).start()
+                    back[1] = result_of(PART)
+                    ret_copy(1, partner).start()
+
             far_copy(c).wait_recv()
             normalize(FAR, start, piece)
             pair(FAR, start, piece, OWN, 0, rows)
@@ -282,24 +304,17 @@
                 if c:
                     pair(ZED, 0, start, FAR, start, piece)
 
-        back[2] = result_of(WHY)
         back[3] = result_of(FAR)
 
         @pl.when(first)
         def _():
-            ret_copy(2, me - 2).start()
             pltpu.make_async_remote_copy(
                 src_ref=back.at[3], dst_ref=ret.at[2], send_sem=ret_send.at[3], recv_sem=ret_recv.at[2],
                 device_id=dev(me - 1), device_id_type=MESH).start()
 
         @pl.when(second)
         def _():
-            pltpu.make_async_remote_copy(
-                src_ref=back.at[2], dst_ref=ret.at[3], send_sem=ret_send.at[2], recv_sem=ret_recv.at[3],
-                device_id=dev(me - 2), device_id_type=MESH).start()
             ret_copy(3, me - 3).start()
-            back[1] = result_of(PART)
-            ret_copy(1, partner).start()
 
         @pl.when(has_down)
         def _():
@@ -361,14 +376,16 @@
     order = order.reshape(-1, LANES)
     result = pl.pallas_call(
         functools.partial(kernel, devices),
-        out_shape=jax.ShapeDtypeStruct((1, rows), jnp.float32),
+        out_shape=pltpu.VMEM((1, rows), jnp.float32),
         in_specs=[
             pl.BlockSpec(memory_space=pl.ANY),
-            pl.BlockSpec(memory_space=pltpu.SMEM),
-            pl.BlockSpec(memory_space=pltpu.VMEM),
+            pl.BlockSpec(memory_space=pl.ANY),
+            pl.BlockSpec(memory_space=pl.ANY),
         ],
         out_specs=pl.BlockSpec(memory_space=pltpu.VMEM),
         scratch_shapes=[
+            pltpu.SMEM(sizes.shape, jnp.int32),
+            pltpu.VMEM(order.shape, jnp.int32),
             pltpu.VMEM((5, rows, width), jnp.bfloat16),
             pltpu.VMEM((5, rows, width), jnp.bfloat16),
             pltpu.VMEM((6, rows, LANES), jnp.float32),
@@ -377,6 +394,7 @@
             pltpu.VMEM((4, 1, rows), jnp.float32),
             pltpu.VMEM((4, 1, rows), jnp.float32),
             pltpu.SemaphoreType.DMA,
+            pltpu.SemaphoreType.DMA((2,)),
             pltpu.SemaphoreType.DMA((5, CHUNKS)),
             pltpu.SemaphoreType.DMA((5, CHUNKS)),
             pltpu.SemaphoreType.DMA((4,)),

time: 24.5 us -> 22.3 us (0.910)
  Pallas kernels: 22.9 us -> 21.6 us
  local copies, waits for them, and re-layouts: 1.26 us -> 0.58 us
    pallas_call x1, Pallas kernels: 22.9 us -> 21.6 us  [local(): pl.pallas_call(functools.partial(kernel, devices), out_shape=pltpu.VMEM((...]
    unnamed x1, local copies, waits for them, and re-layouts: 1.26 us -> 0.58 us
where the time goes in v2:
time: 22.3 us; the launch traced here: 22.2 us
  Pallas kernels  21.6 us (97%)
  local copies, waits for them, and re-layouts  0.58 us (3%)
    pallas_call x1, Pallas kernels, local(): pl.pallas_call(functools.partial(kernel, devices), out_shape=pltpu.VMEM((...  21.6 us
    unnamed x1, local copies, waits for them, and re-layouts  0.58 us

profile of v2, /device:TPU:12, one launch (start us, length us, event | category | flops | bytes accessed | tf_op | source)
XLA Modules:
  0.0 22.2 jit_solution(15871510353674337194)
XLA Ops:
  0.0 21.6 %shard_map.37 = f32[1,512]{1,0:T(1,128)S(1)} custom-call(bf16[512,512]{1,0:T(8,128)(2,1)} %x_ref.1, s32[32]{0:T(128)} %sizes_hbm.1, s32[64,128]{1,0:T(8,128)} %bitcast.3), custom_call_target="tpu_custom_call" | custom-call | tf_op jit(solution)/shard_map/pallas_call | solution.py:377
  21.6 0.6 %copy.5 = f32[512]{0:T(512)} copy(f32[512]{0:T(512)S(1)} %bitcast.2) | data formatting | bytes 4096

commit v3 on v2

--- a/solution.py
+++ b/solution.py
@@ -62,12 +62,14 @@
     load_order.start()
     pl.semaphore_wait(barrier, 3 + has_down.astype(jnp.int32) + has_up.astype(jnp.int32))
 
+    load.wait()
+
     def chunk(c):
         return pl.ds(c * piece, piece)
 
     def own_copy(slot, c, target):
         return pltpu.make_async_remote_copy(
-            src_ref=x_ref.at[chunk(c)], dst_ref=raw.at[slot, chunk(c)],
+            src_ref=raw.at[OWN, chunk(c)], dst_ref=raw.at[slot, chunk(c)],
             send_sem=send_sem.at[slot, c], recv_sem=recv_sem.at[slot, c],
             device_id=dev(target), device_id_type=MESH)
 
@@ -79,7 +81,7 @@
 
     def part_copy():
         return pltpu.make_async_remote_copy(
-            src_ref=x_ref, dst_ref=raw.at[PART],
+            src_ref=raw.at[OWN], dst_ref=raw.at[PART],
             send_sem=send_sem.at[PART, 0], recv_sem=recv_sem.at[PART, 0],
             device_id=dev(partner), device_id_type=MESH)
 
@@ -97,14 +99,15 @@
     takes_part = core == is_b
     sent = []
 
-    for c in range(CHUNKS):
-        @pl.when(sends_z)
-        def _():
+    @pl.when(on_a)
+    def _():
+        for c in range(CHUNKS):
+            own_copy(WHY, c, me + 2).start()
+
+    @pl.when(sends_z)
+    def _():
+        for c in range(CHUNKS):
             own_copy(ZED, c, z_target).start()
-
-        @pl.when(on_a)
-        def _():
-            own_copy(WHY, c, me + 2).start()
 
     @pl.when(sends_part)
     def _():
@@ -239,7 +242,6 @@
             pieces.append(best)
         return jnp.concatenate(pieces, axis=1)
 
-    load.wait()
     normalize(OWN, 0, rows)
     within_own()
 

time: 22.3 us -> 22.1 us (level)
    pallas_call x1, Pallas kernels: 21.6 us -> 21.4 us  [local(): pl.pallas_call(functools.partial(kernel, devices), out_shape=pltpu.VMEM((...]
where the time goes in v3:
time: 22.1 us; the launch traced here: 21.9 us
  Pallas kernels  21.4 us (97%)
  local copies, waits for them, and re-layouts  0.58 us (3%)
    pallas_call x1, Pallas kernels, local(): pl.pallas_call(functools.partial(kernel, devices), out_shape=pltpu.VMEM((...  21.4 us
    unnamed x1, local copies, waits for them, and re-layouts  0.58 us

profile of v3, /device:TPU:12, one launch (start us, length us, event | category | flops | bytes accessed | tf_op | source)
XLA Modules:
  0.0 21.9 jit_solution(11018345136300672428)
XLA Ops:
  0.0 21.4 %shard_map.37 = f32[1,512]{1,0:T(1,128)S(1)} custom-call(bf16[512,512]{1,0:T(8,128)(2,1)} %x_ref.1, s32[32]{0:T(128)} %sizes_hbm.1, s32[64,128]{1,0:T(8,128)} %bitcast.3), custom_call_target="tpu_custom_call" | custom-call | tf_op jit(solution)/shard_map/pallas_call | solution.py:379
  21.4 0.6 %copy.5 = f32[512]{0:T(512)} copy(f32[512]{0:T(512)S(1)} %bitcast.2) | data formatting | bytes 4096

commit v4 on v2

--- a/solution.py
+++ b/solution.py
@@ -60,56 +60,7 @@
     load_sizes.start()
     load_order = pltpu.make_async_copy(order_hbm, order_ref, small_sem.at[1])
     load_order.start()
-    pl.semaphore_wait(barrier, 3 + has_down.astype(jnp.int32) + has_up.astype(jnp.int32))
-
-    def chunk(c):
-        return pl.ds(c * piece, piece)
-
-    def own_copy(slot, c, target):
-        return pltpu.make_async_remote_copy(
-            src_ref=x_ref.at[chunk(c)], dst_ref=raw.at[slot, chunk(c)],
-            send_sem=send_sem.at[slot, c], recv_sem=recv_sem.at[slot, c],
-            device_id=dev(target), device_id_type=MESH)
-
-    def far_copy(c):
-        return pltpu.make_async_remote_copy(
-            src_ref=raw.at[WHY, chunk(c)], dst_ref=raw.at[FAR, chunk(c)],
-            send_sem=send_sem.at[FAR, c], recv_sem=recv_sem.at[FAR, c],
-            device_id=dev(partner), device_id_type=MESH)
-
-    def part_copy():
-        return pltpu.make_async_remote_copy(
-            src_ref=x_ref, dst_ref=raw.at[PART],
-            send_sem=send_sem.at[PART, 0], recv_sem=recv_sem.at[PART, 0],
-            device_id=dev(partner), device_id_type=MESH)
-
-    def ret_copy(slot, target):
-        return pltpu.make_async_remote_copy(
-            src_ref=back.at[slot], dst_ref=ret.at[slot],
-            send_sem=ret_send.at[slot], recv_sem=ret_recv.at[slot],
-            device_id=dev(target), device_id_type=MESH)
-
-    z_target = jnp.where(on_b, me + 4, me - 4)
     z_source = jnp.where(on_b, me - 4, me + 4)
-    sends_z = jnp.where(on_b, has_up, has_down)
-    takes_z = jnp.where(on_b, has_down, has_up)
-    sends_part = core == is_a
-    takes_part = core == is_b
-    sent = []
-
-    for c in range(CHUNKS):
-        @pl.when(sends_z)
-        def _():
-            own_copy(ZED, c, z_target).start()
-
-        @pl.when(on_a)
-        def _():
-            own_copy(WHY, c, me + 2).start()
-
-    @pl.when(sends_part)
-    def _():
-        part_copy().start()
-
     load_sizes.wait()
     load_order.wait()
 
@@ -162,6 +113,58 @@
         col[5, pl.ds(t * LANES, LANES), :] = spread(rank_row(OWN, t))
     acc_low[...] = jnp.full(acc_low.shape, -1.0, jnp.float32)
     acc_high[...] = jnp.full(acc_high.shape, -1.0, jnp.float32)
+
+    pl.semaphore_wait(barrier, 3 + has_down.astype(jnp.int32) + has_up.astype(jnp.int32))
+
+    load.wait()
+
+    def chunk(c):
+        return pl.ds(c * piece, piece)
+
+    def own_copy(slot, c, target):
+        return pltpu.make_async_remote_copy(
+            src_ref=raw.at[OWN, chunk(c)], dst_ref=raw.at[slot, chunk(c)],
+            send_sem=send_sem.at[slot, c], recv_sem=recv_sem.at[slot, c],
+            device_id=dev(target), device_id_type=MESH)
+
+    def far_copy(c):
+        return pltpu.make_async_remote_copy(
+            src_ref=raw.at[WHY, chunk(c)], dst_ref=raw.at[FAR, chunk(c)],
+            send_sem=send_sem.at[FAR, c], recv_sem=recv_sem.at[FAR, c],
+            device_id=dev(partner), device_id_type=MESH)
+
+    def part_copy():
+        return pltpu.make_async_remote_copy(
+            src_ref=raw.at[OWN], dst_ref=raw.at[PART],
+            send_sem=send_sem.at[PART, 0], recv_sem=recv_sem.at[PART, 0],
+            device_id=dev(partner), device_id_type=MESH)
+
+    def ret_copy(slot, target):
+        return pltpu.make_async_remote_copy(
+            src_ref=back.at[slot], dst_ref=ret.at[slot],
+            send_sem=ret_send.at[slot], recv_sem=ret_recv.at[slot],
+            device_id=dev(target), device_id_type=MESH)
+
+    z_target = jnp.where(on_b, me + 4, me - 4)
+    sends_z = jnp.where(on_b, has_up, has_down)
+    takes_z = jnp.where(on_b, has_down, has_up)
+    sends_part = core == is_a
+    takes_part = core == is_b
+    sent = []
+
+    @pl.when(on_a)
+    def _():
+        for c in range(CHUNKS):
+            own_copy(WHY, c, me + 2).start()
+
+    @pl.when(sends_z)
+    def _():
+        for c in range(CHUNKS):
+            own_copy(ZED, c, z_target).start()
+
+    @pl.when(sends_part)
+    def _():
+        part_copy().start()
 
     def normalize(slot, start, count):
         at = pl.ds(start, count)
@@ -239,7 +242,6 @@
             pieces.append(best)
         return jnp.concatenate(pieces, axis=1)
 
-    load.wait()
     normalize(OWN, 0, rows)
     within_own()
 

time: 22.3 us -> 22.1 us (level)
    pallas_call x1, Pallas kernels: 21.6 us -> 21.4 us  [local(): pl.pallas_call(functools.partial(kernel, devices), out_shape=pltpu.VMEM((...]
where the time goes in v4:
time: 22.1 us; the launch traced here: 21.9 us
  Pallas kernels  21.4 us (97%)
  local copies, waits for them, and re-layouts  0.58 us (3%)
    pallas_call x1, Pallas kernels, local(): pl.pallas_call(functools.partial(kernel, devices), out_shape=pltpu.VMEM((...  21.4 us
    unnamed x1, local copies, waits for them, and re-layouts  0.58 us

profile of v4, /device:TPU:12, one launch (start us, length us, event | category | flops | bytes accessed | tf_op | source)
XLA Modules:
  0.0 21.9 jit_solution(8280968097148881040)
XLA Ops:
  0.0 21.4 %shard_map.37 = f32[1,512]{1,0:T(1,128)S(1)} custom-call(bf16[512,512]{1,0:T(8,128)(2,1)} %x_ref.1, s32[32]{0:T(128)} %sizes_hbm.1, s32[64,128]{1,0:T(8,128)} %bitcast.3), custom_call_target="tpu_custom_call" | custom-call | tf_op jit(solution)/shard_map/pallas_call | solution.py:379
  21.4 0.6 %copy.5 = f32[512]{0:T(512)} copy(f32[512]{0:T(512)S(1)} %bitcast.2) | data formatting | bytes 4096
